TPU v7x, 256 devices: a whole 4x4x8 slice. The times are simulated.
256 devices in a mesh: row: 8 (over y, core), col: 32 (over z, x).
Axes of the slice: x: 4, y: 4, z: 8, core: 2. Of those that a mesh axis runs over, the one named last changes fastest.
Arguments:
- diag_block: float32 [1024, 1024], P('row')
- panel: bfloat16 [64, 1024, 1024], P('col', 'row'), may hold values from -1 to 1
- trailing: bfloat16 [32, 12, 1024, 1024], P('col', None, 'row'), may hold values from -6 to 6
- slot_rows: int32 [32, 12], replicated, may hold values from -1 to 63, as said below
- slot_cols: int32 [32, 12], replicated, may hold values from 0 to 1, as said below
Outputs:
- panel_factor: bfloat16 [64, 1024, 1024], P('col', 'row')
- updated: bfloat16 [32, 12, 1024, 1024], P('col', None, 'row')
Inputs may be any that keep to these rules, and one draw needn't show every extreme that they name: Slot s of grid column c holds the tile at tile row slot_rows[c, s] and tile column 2 * c + slot_cols[c, s] of the trailing matrix, or nothing where slot_rows[c, s] is -1. Live slots come first in each column; the pairs of one column are distinct and lie on or below the diagonal (tile row at least tile column). Within one grid column, live slots whose tile rows a and a' have a // 2 == a' // 2 have a == a'. Every column holds at least one live slot, column 0 fills all 12 slots and column 16 holds exactly one. `slot_cols`: 0 in empty slots.
All inputs are finite; a program needn't handle non-finite values.
Results may differ from a plain program's by a relative error of at most 0.0019.
Values may be sent and summed in bfloat16 or wider, within the bound.
No kernel may reach another device: no remote copies, remote signals or barrier semaphores. Data moves between devices by JAX's collectives and lax.ppermute only.
A program may use at most 128 MiB of HBM per device.

v0:
```python
import jax
import jax.numpy as jnp
from jax import lax
from jax.sharding import PartitionSpec as P


def slot_product(slices, left_ids, source_tiles, col_ids, position):
    left_slice = lax.dynamic_index_in_dim(slices, left_ids[position], 0, keepdims=False)
    right_tile = lax.dynamic_index_in_dim(source_tiles, col_ids[position], 0, keepdims=False)
    return lax.dot_general(
        left_slice, right_tile, (((1,), (1,)), ((), ())), preferred_element_type=jnp.float32
    )


def subtract_slot(buffer, position, update):
    previous = lax.dynamic_index_in_dim(buffer, position, 0, keepdims=False).astype(jnp.float32)
    return lax.dynamic_update_index_in_dim(
        buffer, (previous - update).astype(jnp.bfloat16), position, 0
    )


def local(diag_block, panel, trailing, slot_rows, slot_cols):
    diag_full = lax.all_gather(diag_block, "row", axis=0, tiled=True)
    factor = jnp.linalg.cholesky(diag_full)
    tile_count, row_count, tile_width = panel.shape
    stacked = panel.astype(jnp.float32).reshape(tile_count * row_count, tile_width)
    solved = lax.linalg.triangular_solve(factor, stacked.T, left_side=True, lower=True)
    panel_factor = solved.T.reshape(tile_count, row_count, tile_width).astype(jnp.bfloat16)
    whole_tiles = lax.all_gather(panel_factor, "row", axis=1, tiled=True)
    column_index = lax.axis_index("col")
    own_rows = lax.dynamic_index_in_dim(slot_rows, column_index, 0, keepdims=False)
    own_cols = lax.dynamic_index_in_dim(slot_cols, column_index, 0, keepdims=False)
    own_count = jnp.sum((own_rows >= 0).astype(jnp.int32))
    slices = lax.all_gather(panel_factor, "col", axis=0, tiled=True)

    def own_step(position, buffer):
        return subtract_slot(
            buffer, position, slot_product(slices, own_rows, whole_tiles, own_cols, position)
        )

    buffer = lax.fori_loop(0, own_count, own_step, trailing[0])
    return (panel_factor, buffer[None])


def solution(mesh):
    return jax.shard_map(
        local,
        mesh=mesh,
        in_specs=(P("row", None), P("col", "row", None), P("col", None, "row", None), P(), P()),
        out_specs=(P("col", "row", None), P("col", None, "row", None)),
        check_vma=False,
    )
```

profile of v0, /device:TPU:1, one launch (start us, length us, event | category | flops | bytes accessed | tf_op | source)
XLA Modules:
  0.0 681.8 jit_solution(6531067428901336610)
XLA Ops:
  9.6 43.7 %all-gather.4.cloned.1.call-done = f32[1024,1024]{0,1:T(8,128)} async-done(((f32[128,1024]{0,1:T(8,128)}), f32[1024,1024]{0,1:T(8,128)}) %all-gather.4.cloned.1.call-update) | async-done | bytes 4194320 | tf_op jit(solution)/shard_map/all_gather | solution.py:23
  53.3 5.3 copy.18
  58.7 4.4 fusion.18
  63.1 1.9 copy-done
  65.0 11.7 %cholesky.223 = f32[128,128]{1,0:T(8,128)S(1)} custom-call(f32[128,128]{1,0:T(8,128)S(1)} %cholesky.580), custom_call_target="Cholesky" | custom-call | tf_op jit(solution)/shard_map/jit(cholesky)/cholesky | solution.py:24
  76.8 9.8 %custom-call.62 = f32[1,128,128]{1,2,0:T(8,128)S(1)} custom-call(f32[1,128,128]{2,1,0:T(8,128)S(1)} %get-tuple-element.117), custom_call_target="InvertDiagBlocksLowerTriangular" | custom-call | tf_op jit(solution)/shard_map/jit(cholesky)/cholesky | solution.py:24
  86.6 2.5 cholesky.255
  89.1 2.4 constant_dynamic-update-slice_fusion.24
  91.5 1.5 convolution_subtract_fusion
  93.0 12.2 %cholesky.244 = f32[128,128]{1,0:T(8,128)S(1)} custom-call(f32[128,128]{1,0:T(8,128)S(1)} %cholesky.584), custom_call_target="Cholesky" | custom-call | tf_op jit(solution)/shard_map/jit(cholesky)/cholesky | solution.py:24
  105.8 9.8 %custom-call.63 = f32[1,128,128]{1,2,0:T(8,128)S(1)} custom-call(f32[1,128,128]{2,1,0:T(8,128)S(1)} %get-tuple-element.114), custom_call_target="InvertDiagBlocksLowerTriangular" | custom-call | tf_op jit(solution)/shard_map/jit(cholesky)/cholesky | solution.py:24
  116.9 2.1 convolution_subtract_fusion.1
  119.0 11.7 %cholesky.468 = f32[128,128]{1,0:T(8,128)S(1)} custom-call(f32[128,128]{1,0:T(8,128)S(1)} %cholesky.589), custom_call_target="Cholesky" | custom-call | tf_op jit(solution)/shard_map/jit(cholesky)/cholesky | solution.py:24
  132.0 9.8 %custom-call.64 = f32[1,128,128]{1,2,0:T(8,128)S(1)} custom-call(f32[1,128,128]{2,1,0:T(8,128)S(1)} %get-tuple-element.111), custom_call_target="InvertDiagBlocksLowerTriangular" | custom-call | tf_op jit(solution)/shard_map/jit(cholesky)/cholesky | solution.py:24
  143.0 2.3 convolution_subtract_fusion.2
  145.3 11.8 %cholesky.487 = f32[128,128]{1,0:T(8,128)S(1)} custom-call(f32[128,128]{1,0:T(8,128)S(1)} %cholesky.594), custom_call_target="Cholesky" | custom-call | tf_op jit(solution)/shard_map/jit(cholesky)/cholesky | solution.py:24
  158.5 9.8 %custom-call.65 = f32[1,128,128]{1,2,0:T(8,128)S(1)} custom-call(f32[1,128,128]{2,1,0:T(8,128)S(1)} %get-tuple-element.108), custom_call_target="InvertDiagBlocksLowerTriangular" | custom-call | tf_op jit(solution)/shard_map/jit(cholesky)/cholesky | solution.py:24
  169.4 2.3 convolution_subtract_fusion.3
  171.7 11.7 %cholesky.506 = f32[128,128]{1,0:T(8,128)S(1)} custom-call(f32[128,128]{1,0:T(8,128)S(1)} %cholesky.599), custom_call_target="Cholesky" | custom-call | tf_op jit(solution)/shard_map/jit(cholesky)/cholesky | solution.py:24
  184.7 10.0 %custom-call.66 = f32[1,128,128]{1,2,0:T(8,128)S(1)} custom-call(f32[1,128,128]{2,1,0:T(8,128)S(1)} %get-tuple-element.105), custom_call_target="InvertDiagBlocksLowerTriangular" | custom-call | tf_op jit(solution)/shard_map/jit(cholesky)/cholesky | solution.py:24
  195.8 2.3 convolution_subtract_fusion.4
  198.1 11.7 %cholesky.526 = f32[128,128]{1,0:T(8,128)S(1)} custom-call(f32[128,128]{1,0:T(8,128)S(1)} %cholesky.604), custom_call_target="Cholesky" | custom-call | tf_op jit(solution)/shard_map/jit(cholesky)/cholesky | solution.py:24
  211.0 9.8 %custom-call.67 = f32[1,128,128]{1,2,0:T(8,128)S(1)} custom-call(f32[1,128,128]{2,1,0:T(8,128)S(1)} %get-tuple-element.102), custom_call_target="InvertDiagBlocksLowerTriangular" | custom-call | tf_op jit(solution)/shard_map/jit(cholesky)/cholesky | solution.py:24
  221.7 2.0 convolution_subtract_fusion.11
  223.8 12.1 %cholesky.546 = f32[128,128]{1,0:T(8,128)S(1)} custom-call(f32[128,128]{1,0:T(8,128)S(1)} %cholesky.609), custom_call_target="Cholesky" | custom-call | tf_op jit(solution)/shard_map/jit(cholesky)/cholesky | solution.py:24
  237.2 9.8 %custom-call.68 = f32[1,128,128]{1,2,0:T(8,128)S(1)} custom-call(f32[1,128,128]{2,1,0:T(8,128)S(1)} %get-tuple-element.99), custom_call_target="InvertDiagBlocksLowerTriangular" | custom-call | tf_op jit(solution)/shard_map/jit(cholesky)/cholesky | solution.py:24
  247.9 1.8 convolution_subtract_fusion.13
  249.7 11.7 %cholesky.564 = f32[128,128]{1,0:T(8,128)S(1)} custom-call(f32[128,128]{1,0:T(8,128)S(1)} %convolution_subtract_fusion.13), custom_call_target="Cholesky" | custom-call | tf_op jit(solution)/shard_map/jit(cholesky)/cholesky | solution.py:24
  268.3 4.8 select_select_fusion
  273.1 23.0 %while.12 = (s32[]{:T(128)}, f32[1024,1024]{1,0:T(8,128)}, s32[8,2]{0,1:T(2,128)S(1)}, f32[8,128,128]{2,1,0:T(8,128)S(1)}, s32[]{:T(128)}) while((s32[]{:T(128)}, f32[1024,1024]{1,0:T(8,128)}, s32[8,2]{0,1:T(2,128)S(1)}, f32[8,128,128]{2,1,0:T(8,128)S(1)}, s32[]{:T(128)}) %tuple.74), condition=%wide.while_cond, body=%wide.while_body.sunk | while | flops 2 | bytes 131189 | solution.py:27
  273.7 2.3 bitcast_dynamic-update-slice_fusion.2
  276.6 2.3 bitcast_dynamic-update-slice_fusion.2
  279.5 2.3 bitcast_dynamic-update-slice_fusion.2
  282.4 2.3 bitcast_dynamic-update-slice_fusion.2
  285.2 2.3 bitcast_dynamic-update-slice_fusion.2
  288.1 2.3 bitcast_dynamic-update-slice_fusion.2
  291.0 2.3 bitcast_dynamic-update-slice_fusion.2
  293.9 2.2 bitcast_dynamic-update-slice_fusion.2
  296.1 78.8 %custom-call.69 = f32[8,128,128]{1,2,0:T(8,128)S(1)} custom-call(f32[8,128,128]{2,1,0:T(8,128)S(1)} %get-tuple-element.48), custom_call_target="InvertDiagBlocksLowerTriangular" | custom-call | tf_op jit(solution)/shard_map/triangular_solve | solution.py:27
  380.0 1.3 convolution_subtract_fusion.7
  382.2 1.4 convolution_subtract_fusion.6
  384.7 1.7 convolution_subtract_fusion.5
  386.4 1.8 convert_dynamic-update-slice_fusion.1
  388.2 1.5 convolution_subtract_fusion.9
  389.7 1.8 convert_dynamic-update-slice_fusion
  391.5 1.7 convolution_subtract_fusion.12
  393.2 1.8 fusion.19
  394.9 2.0 copy.24
  398.6 34.2 %all-gather.8.cloned.1.call-done = bf16[2,1024,1024]{2,1,0:T(8,128)(2,1)} async-done(((bf16[2,128,1024]{2,1,0:T(8,128)(2,1)}), bf16[2,1024,1024]{2,1,0:T(8,128)(2,1)}) %all-gather.8.cloned.1.call-update) | async-done | bytes 4194320 | tf_op jit(solution)/shard_map/all_gather | solution.py:29
  432.8 142.9 %all-gather.6.cloned.1.call-done = bf16[64,128,1024]{2,1,0:T(8,128)(2,1)} async-done(((bf16[2,128,1024]{2,1,0:T(8,128)(2,1)}), bf16[64,128,1024]{2,1,0:T(8,128)(2,1)}) %all-gather.6.cloned.1.call-update) | async-done | bytes 16777232 | tf_op jit(solution)/shard_map/all_gather | solution.py:34
  575.8 97.6 %while.11 = (s32[]{:T(128)}, bf16[12,128,1024]{2,1,0:T(8,128)(2,1)S(1)}, s32[]{:T(128)}, s32[12]{0:T(128)S(1)}, bf16[64,128,1024]{2,1,0:T(8,128)(2,1)}, /*index=...) while((s32[]{:T(128)}, ...), condition=%wide.region_18.19_spmd, body=%wide.region_17.18_spmd.sunk | while | flops 268828672 | bytes 3408139 | solution.py:41
  581.3 2.5 fusion.100
  589.4 2.5 fusion.100
  597.5 2.5 fusion.100
  605.6 2.5 fusion.100
  613.6 2.5 fusion.100
  621.7 2.5 fusion.100
  629.8 2.5 fusion.100
  637.9 2.5 fusion.100
  646.0 2.5 fusion.100
  654.1 2.5 fusion.100
  662.1 2.5 fusion.100
  670.2 2.5 fusion.100
  673.4 1.7 copy-done.1
  (124 shorter events, 45.9 us)
Async XLA Ops:
  7.2 1.0 copy-start.4
  7.2 2.1 copy-start.5
  7.2 46.1 %all-gather.4.cloned.1.call-start = ((), (), s32[]{:S(2)}) async-start(), calls=%async_computation | async-start | bytes 4718592 | tf_op jit(solution)/shard_map/all_gather | solution.py:23
  9.2 423.6 %all-gather.8.cloned.1.call-start = ((), (), s32[]{:S(2)}) async-start(), calls=%async_computation.2 | async-start | bytes 4718592 | tf_op jit(solution)/shard_map/all_gather | solution.py:29
  9.6 372.6 %copy-start.3 = (f32[1024,256]{1,0:T(8,128)}, f32[1024,256]{1,0:T(8,128)S(1)}, u32[]{:S(2)}) copy-start(f32[1024,256]{1,0:T(8,128)S(1)} %bitcast_convert_fusion) | copy-start | bytes 3145732
  63.1 1.9 copy-start
  374.9 9.7 %copy-start.6 = (f32[8,128,128]{1,2,0:T(8,128)}, f32[8,128,128]{1,2,0:T(8,128)S(1)}, u32[]{:S(2)}) copy-start(f32[8,128,128]{1,2,0:T(8,128)S(1)} %custom-call.69) | copy-start | bytes 1572868
  384.7 13.1 %copy-start.7 = (s32[32,12]{0,1:T(8,128)S(1)}, s32[32,12]{0,1:T(8,128)}, u32[]{:S(2)}) copy-start(s32[32,12]{0,1:T(8,128)} %param.11) | copy-start | bytes 4612
  384.7 13.1 %copy-start.8 = (s32[32,12]{0,1:T(8,128)S(1)}, s32[32,12]{0,1:T(8,128)}, u32[]{:S(2)}) copy-start(s32[32,12]{0,1:T(8,128)} %param.10) | copy-start | bytes 4612
  384.7 191.1 %copy-start.2 = (bf16[1,12,128,1024]{3,2,1,0:T(8,128)(2,1)S(1)}, bf16[1,12,128,1024]{3,2,1,0:T(8,128)(2,1)}, u32[]{:S(2)}) copy-start(bf16[1,12,128,1024]{3,2,1,0:T(8,128)(2,1)} %param.9) | copy-start | bytes 9437188
  397.0 178.7 %all-gather.6.cloned.1.call-start = ((), (), s32[]{:S(2)}) async-start(), calls=%async_computation.1 | async-start | bytes 17301504 | tf_op jit(solution)/shard_map/all_gather | solution.py:34
  673.4 1.7 copy-start.1
Sparse Core Ops, SparseCore 0:
  10.4 42.8 all-gather.3
  397.1 35.6 all-gather.7
  436.0 139.6 all-gather.5
where the time goes:
time: 693 us; the launch traced here: 682 us
  other arithmetic  261 us (38%)
  waiting for transfers between devices  222 us (32%)
  matrix products  73.2 us (11%)
  local copies, waits for them, and re-layouts  53.5 us (8%)
  loops' own time  52.9 us (8%)
  between operations  19.3 us (3%)
    another operation x30, other arithmetic, local(): factor = jnp.linalg.cholesky(diag_full)  173 us
    all_gather x1, waiting for transfers between devices, local(): slices = lax.all_gather(panel_factor, 'col', axis=0, tiled=True)  143 us
    another operation x3, other arithmetic, local(): lax.linalg.triangular_solve(factor, stacked.T, left_side=True, lower=True)  83.6 us
    another operation x1, loops' own time, local(): buffer = lax.fori_loop(0, own_count, own_step, trailing[0])  52.7 us
    all_gather x1, waiting for transfers between devices, local(): diag_full = lax.all_gather(diag_block, 'row', axis=0, tiled=True)  43.7 us
    all_gather x1, waiting for transfers between devices, local(): whole_tiles = lax.all_gather(panel_factor, 'row', axis=1, tiled=True)  34.2 us
    dot_general x12, matrix products, slot_product(): lax.dot_general(left_slice, right_tile, (((1,), (1,)), ((), ())), preferr...  30.3 us
    another operation x14, matrix products, local(): factor = jnp.linalg.cholesky(diag_full)  23.1 us
  transfers between devices with their start and end apart: 3, of which 3 were waited for; matrix products, arithmetic and copies ran while one was open for 0% of the time, Pallas kernels for 0%

commit v1 on v0

--- a/solution.py
+++ b/solution.py
@@ -26,7 +26,9 @@
     stacked = panel.astype(jnp.float32).reshape(tile_count * row_count, tile_width)
     solved = lax.linalg.triangular_solve(factor, stacked.T, left_side=True, lower=True)
     panel_factor = solved.T.reshape(tile_count, row_count, tile_width).astype(jnp.bfloat16)
-    whole_tiles = lax.all_gather(panel_factor, "row", axis=1, tiled=True)
+    whole_tiles = jnp.concatenate(
+        lax.all_to_all(jnp.stack([panel_factor] * lax.axis_size("row")), "row", 0, 0), axis=1
+    )
     column_index = lax.axis_index("col")
     own_rows = lax.dynamic_index_in_dim(slot_rows, column_index, 0, keepdims=False)
     own_cols = lax.dynamic_index_in_dim(slot_cols, column_index, 0, keepdims=False)

time: 693 us -> 647 us (0.934)
  waiting for transfers between devices: 222 us -> 171 us
  matrix products: 73.2 us -> 65.4 us
  local copies, waits for them, and re-layouts: 53.5 us -> 61.3 us
    all_gather x1, waiting for transfers between devices: 143 us -> 78.9 us  [local(): slices = lax.all_gather(panel_factor, 'col', axis=0, tiled=True)]
    all_to_all x0 -> x1, waiting for transfers between devices: none -> 48.1 us  [local(): lax.all_to_all(jnp.stack([panel_factor] * lax.axis_size('row')), 'row', 0...]
    all_gather x1 -> x0, waiting for transfers between devices: 34.2 us -> none  [local(): whole_tiles = lax.all_gather(panel_factor, 'row', axis=1, tiled=True)]
    another operation x15, matrix products: 19.7 us -> 12 us  [local(): lax.linalg.triangular_solve(factor, stacked.T, left_side=True, lower=True)]
    another operation x24 -> x25, local copies, waits for them, and re-layouts: 22.8 us -> 26.3 us
  transfers between devices with their start and end apart: 3 -> 3, of which waited for: 3 -> 3; matrix products, arithmetic and copies ran while one was open for 0% -> 1% of each run, Pallas kernels for 0% -> 0%
where the time goes in v1:
time: 647 us; the launch traced here: 636 us
  other arithmetic  261 us (40%)
  waiting for transfers between devices  171 us (26%)
  matrix products  65.4 us (10%)
  local copies, waits for them, and re-layouts  61.3 us (9%)
  loops' own time  52.7 us (8%)
  between operations  19.5 us (3%)
    another operation x30, other arithmetic, local(): factor = jnp.linalg.cholesky(diag_full)  172 us
    another operation x3, other arithmetic, local(): lax.linalg.triangular_solve(factor, stacked.T, left_side=True, lower=True)  83.6 us
    all_gather x1, waiting for transfers between devices, local(): slices = lax.all_gather(panel_factor, 'col', axis=0, tiled=True)  78.9 us
    another operation x1, loops' own time, local(): buffer = lax.fori_loop(0, own_count, own_step, trailing[0])  52.5 us
    all_to_all x1, waiting for transfers between devices, local(): lax.all_to_all(jnp.stack([panel_factor] * lax.axis_size('row')), 'row', 0...  48.1 us
    all_gather x1, waiting for transfers between devices, local(): diag_full = lax.all_gather(diag_block, 'row', axis=0, tiled=True)  43.7 us
    dot_general x12, matrix products, slot_product(): lax.dot_general(left_slice, right_tile, (((1,), (1,)), ((), ())), preferr...  30.3 us
    another operation x14, matrix products, local(): factor = jnp.linalg.cholesky(diag_full)  23.1 us
  transfers between devices with their start and end apart: 3, of which 3 were waited for; matrix products, arithmetic and copies ran while one was open for 1% of the time, Pallas kernels for 0%

profile of v1, /device:TPU:1, one launch (start us, length us, event | category | flops | bytes accessed | tf_op | source)
XLA Modules:
  0.0 635.8 jit_solution(16033865440396362444)
XLA Ops:
  9.6 43.7 %all-gather.3.cloned.1.call-done = f32[1024,1024]{0,1:T(8,128)} async-done(((f32[128,1024]{0,1:T(8,128)}), f32[1024,1024]{0,1:T(8,128)}) %all-gather.3.cloned.1.call-update) | async-done | bytes 4194320 | tf_op jit(solution)/shard_map/all_gather | solution.py:23
  53.3 5.3 copy.24
  58.7 4.4 fusion.18
  63.1 1.9 copy-done
  65.0 11.7 %cholesky.223 = f32[128,128]{1,0:T(8,128)S(1)} custom-call(f32[128,128]{1,0:T(8,128)S(1)} %cholesky.580), custom_call_target="Cholesky" | custom-call | tf_op jit(solution)/shard_map/jit(cholesky)/cholesky | solution.py:24
  76.8 9.8 %custom-call.62 = f32[1,128,128]{1,2,0:T(8,128)S(1)} custom-call(f32[1,128,128]{2,1,0:T(8,128)S(1)} %get-tuple-element.119), custom_call_target="InvertDiagBlocksLowerTriangular" | custom-call | tf_op jit(solution)/shard_map/jit(cholesky)/cholesky | solution.py:24
  86.6 2.5 cholesky.255
  89.1 2.4 constant_dynamic-update-slice_fusion.24
  91.5 1.5 convolution_subtract_fusion
  93.0 12.2 %cholesky.244 = f32[128,128]{1,0:T(8,128)S(1)} custom-call(f32[128,128]{1,0:T(8,128)S(1)} %cholesky.584), custom_call_target="Cholesky" | custom-call | tf_op jit(solution)/shard_map/jit(cholesky)/cholesky | solution.py:24
  105.8 9.8 %custom-call.63 = f32[1,128,128]{1,2,0:T(8,128)S(1)} custom-call(f32[1,128,128]{2,1,0:T(8,128)S(1)} %get-tuple-element.116), custom_call_target="InvertDiagBlocksLowerTriangular" | custom-call | tf_op jit(solution)/shard_map/jit(cholesky)/cholesky | solution.py:24
  115.6 1.2 convolution_dynamic-update-slice_fusion
  116.9 2.1 convolution_subtract_fusion.1
  119.0 11.7 %cholesky.468 = f32[128,128]{1,0:T(8,128)S(1)} custom-call(f32[128,128]{1,0:T(8,128)S(1)} %cholesky.589), custom_call_target="Cholesky" | custom-call | tf_op jit(solution)/shard_map/jit(cholesky)/cholesky | solution.py:24
  132.0 9.8 %custom-call.64 = f32[1,128,128]{1,2,0:T(8,128)S(1)} custom-call(f32[1,128,128]{2,1,0:T(8,128)S(1)} %get-tuple-element.113), custom_call_target="InvertDiagBlocksLowerTriangular" | custom-call | tf_op jit(solution)/shard_map/jit(cholesky)/cholesky | solution.py:24
  142.9 2.3 convolution_subtract_fusion.2
  145.3 11.8 %cholesky.487 = f32[128,128]{1,0:T(8,128)S(1)} custom-call(f32[128,128]{1,0:T(8,128)S(1)} %cholesky.594), custom_call_target="Cholesky" | custom-call | tf_op jit(solution)/shard_map/jit(cholesky)/cholesky | solution.py:24
  158.4 9.8 %custom-call.65 = f32[1,128,128]{1,2,0:T(8,128)S(1)} custom-call(f32[1,128,128]{2,1,0:T(8,128)S(1)} %get-tuple-element.110), custom_call_target="InvertDiagBlocksLowerTriangular" | custom-call | tf_op jit(solution)/shard_map/jit(cholesky)/cholesky | solution.py:24
  169.3 2.3 convolution_subtract_fusion.3
  171.7 11.7 %cholesky.506 = f32[128,128]{1,0:T(8,128)S(1)} custom-call(f32[128,128]{1,0:T(8,128)S(1)} %cholesky.599), custom_call_target="Cholesky" | custom-call | tf_op jit(solution)/shard_map/jit(cholesky)/cholesky | solution.py:24
  184.7 10.0 %custom-call.66 = f32[1,128,128]{1,2,0:T(8,128)S(1)} custom-call(f32[1,128,128]{2,1,0:T(8,128)S(1)} %get-tuple-element.107), custom_call_target="InvertDiagBlocksLowerTriangular" | custom-call | tf_op jit(solution)/shard_map/jit(cholesky)/cholesky | solution.py:24
  195.7 2.3 convolution_subtract_fusion.4
  198.0 11.7 %cholesky.526 = f32[128,128]{1,0:T(8,128)S(1)} custom-call(f32[128,128]{1,0:T(8,128)S(1)} %cholesky.604), custom_call_target="Cholesky" | custom-call | tf_op jit(solution)/shard_map/jit(cholesky)/cholesky | solution.py:24
  211.0 9.8 %custom-call.67 = f32[1,128,128]{1,2,0:T(8,128)S(1)} custom-call(f32[1,128,128]{2,1,0:T(8,128)S(1)} %get-tuple-element.104), custom_call_target="InvertDiagBlocksLowerTriangular" | custom-call | tf_op jit(solution)/shard_map/jit(cholesky)/cholesky | solution.py:24
  221.7 2.0 convolution_subtract_fusion.11
  223.8 12.1 %cholesky.546 = f32[128,128]{1,0:T(8,128)S(1)} custom-call(f32[128,128]{1,0:T(8,128)S(1)} %cholesky.609), custom_call_target="Cholesky" | custom-call | tf_op jit(solution)/shard_map/jit(cholesky)/cholesky | solution.py:24
  237.1 9.8 %custom-call.68 = f32[1,128,128]{1,2,0:T(8,128)S(1)} custom-call(f32[1,128,128]{2,1,0:T(8,128)S(1)} %get-tuple-element.101), custom_call_target="InvertDiagBlocksLowerTriangular" | custom-call | tf_op jit(solution)/shard_map/jit(cholesky)/cholesky | solution.py:24
  247.8 1.8 convolution_subtract_fusion.13
  249.6 11.7 %cholesky.564 = f32[128,128]{1,0:T(8,128)S(1)} custom-call(f32[128,128]{1,0:T(8,128)S(1)} %convolution_subtract_fusion.13), custom_call_target="Cholesky" | custom-call | tf_op jit(solution)/shard_map/jit(cholesky)/cholesky | solution.py:24
  268.1 4.8 select_select_fusion
  272.9 23.0 %while.12 = (s32[]{:T(128)}, f32[1024,1024]{1,0:T(8,128)}, s32[8,2]{0,1:T(2,128)S(1)}, f32[8,128,128]{2,1,0:T(8,128)S(1)}, s32[]{:T(128)}) while((s32[]{:T(128)}, f32[1024,1024]{1,0:T(8,128)}, s32[8,2]{0,1:T(2,128)S(1)}, f32[8,128,128]{2,1,0:T(8,128)S(1)}, s32[]{:T(128)}) %tuple.75), condition=%wide.while_cond, body=%wide.while_body.sunk | while | flops 2 | bytes 131181 | solution.py:27
  273.5 2.3 bitcast_dynamic-update-slice_fusion.2
  276.4 2.3 bitcast_dynamic-update-slice_fusion.2
  279.3 2.3 bitcast_dynamic-update-slice_fusion.2
  282.2 2.3 bitcast_dynamic-update-slice_fusion.2
  285.0 2.3 bitcast_dynamic-update-slice_fusion.2
  287.9 2.3 bitcast_dynamic-update-slice_fusion.2
  290.8 2.3 bitcast_dynamic-update-slice_fusion.2
  293.7 2.2 bitcast_dynamic-update-slice_fusion.2
  295.9 78.8 %custom-call.69 = f32[8,128,128]{1,2,0:T(8,128)S(1)} custom-call(f32[8,128,128]{2,1,0:T(8,128)S(1)} %get-tuple-element.48), custom_call_target="InvertDiagBlocksLowerTriangular" | custom-call | tf_op jit(solution)/shard_map/triangular_solve | solution.py:27
  377.9 1.3 convolution_subtract_fusion.7
  379.5 1.4 convolution_subtract_fusion.6
  381.4 1.5 convolution_subtract_fusion.5
  383.2 1.5 convolution_subtract_fusion.9
  385.1 1.6 convolution_subtract_fusion.12
  388.1 3.5 stack.2
  391.6 4.8 all-to-all-start
  397.2 48.1 %all-to-all-done = bf16[8,2,128,1024]{3,2,1,0:T(8,128)(2,1)} async-done(((bf16[8,2,128,1024]{3,2,1,0:T(8,128)(2,1)}), bf16[8,2,128,1024]{3,2,1,0:T(8,128)(2,1)}, u32[]{:S(2)}, u32[]{:S(2)}) %all-to-all-start) | async-done | bytes 4194336 | tf_op jit(solution)/shard_map/all_to_all | solution.py:30
  445.3 4.7 copy.28
  450.0 78.9 %all-gather.5.cloned.1.call-done = bf16[64,128,1024]{2,1,0:T(8,128)(2,1)} async-done(((bf16[2,128,1024]{2,1,0:T(8,128)(2,1)}), bf16[64,128,1024]{2,1,0:T(8,128)(2,1)}) %all-gather.5.cloned.1.call-update) | async-done | bytes 16777232 | tf_op jit(solution)/shard_map/all_gather | solution.py:36
  528.9 98.1 %while.11 = (s32[]{:T(128)}, bf16[12,128,1024]{2,1,0:T(8,128)(2,1)S(1)}, s32[]{:T(128)}, s32[12]{0:T(128)S(1)}, bf16[64,128,1024]{2,1,0:T(8,128)(2,1)}, /*index=...) while((s32[]{:T(128)}, ...), condition=%wide.region_18.19_spmd, body=%wide.region_17.18_spmd.sunk | while | flops 268828672 | bytes 3408131 | solution.py:43
  534.5 2.5 fusion.100
  542.7 2.5 fusion.100
  550.8 2.5 fusion.100
  558.9 2.5 fusion.100
  567.0 2.5 fusion.100
  575.2 2.5 fusion.100
  583.3 2.5 fusion.100
  591.4 2.5 fusion.100
  599.5 2.5 fusion.100
  607.7 2.5 fusion.100
  615.8 2.5 fusion.100
  623.9 2.5 fusion.100
  627.1 1.7 copy-done.1
  (121 shorter events, 43.3 us)
Async XLA Ops:
  7.2 1.0 copy-start.3
  7.2 2.1 copy-start.4
  7.2 46.1 %all-gather.3.cloned.1.call-start = ((), (), s32[]{:S(2)}) async-start(), calls=%async_computation.1 | async-start | bytes 4718592 | tf_op jit(solution)/shard_map/all_gather | solution.py:23
  9.2 519.7 %all-gather.5.cloned.1.call-start = ((), (), s32[]{:S(2)}) async-start(), calls=%async_computation.2 | async-start | bytes 17301504 | tf_op jit(solution)/shard_map/all_gather | solution.py:36
  63.1 1.9 copy-start
  391.6 4.8 copy-start.5
  391.6 4.8 copy-start.6
  391.6 53.7 %all-to-all-start = ((bf16[8,2,128,1024]{3,2,1,0:T(8,128)(2,1)}), bf16[8,2,128,1024]{3,2,1,0:T(8,128)(2,1)}, u32[]{:S(2)}, u32[]{:S(2)}) async-start(bf16[8,2,128,1024]{3,2,1,0:T(8,128)(2,1)} %stack.2), calls=%async_computation | async-start | bytes 8388608 | tf_op jit(solution)/shard_map/all_to_all | solution.py:30
  397.2 131.7 %copy-start.2 = (bf16[1,12,128,1024]{3,2,1,0:T(8,128)(2,1)S(1)}, bf16[1,12,128,1024]{3,2,1,0:T(8,128)(2,1)}, u32[]{:S(2)}) copy-start(bf16[1,12,128,1024]{3,2,1,0:T(8,128)(2,1)} %param.9) | copy-start | bytes 9437188
  627.1 1.7 copy-start.1
Sparse Core Ops, SparseCore 0:
  10.4 42.8 all-gather.2
  388.2 140.7 all-gather.4
